TPU v7x, 256 devices: a whole 4x4x8 slice. The times are simulated.
256 devices in a mesh: leaf: 64 (over y, z, core), rows: 4 (over x).
Axes of the slice: x: 4, y: 4, z: 8, core: 2. Of those that a mesh axis runs over, the one named last changes fastest.
Arguments:
- mixing: bfloat16 [192, 1024, 1024], P('leaf'), may hold values from 0.04 to 2048
- emission: bfloat16 [192, 256, 1024], P('leaf'), may hold values from 0.099609375 to 10
- prior: float32 [1024], replicated, may hold values from 0.1 to 10
- parent: int32 [192], P('leaf'), may hold values from -1 to 191, as said below
- observed: int32 [192, 512], P('leaf', 'rows'), may hold values from 0 to 255
Outputs:
- pair_counts: bfloat16 [192, 1024, 1024], P('leaf', 'rows')
- emit_counts: bfloat16 [192, 256, 1024], P('leaf', None, 'rows')
Inputs may be any that keep to these rules, and one draw needn't show every extreme that they name: Nodes are numbered 3 to an index of leaf, in order. Every parent has a smaller number than its child. A node that is not the first of its index of leaf has its parent among the nodes of the same index. The first node of index d > 0 has as parent the first node of index d with its lowest set binary digit cleared. Node 0 is the root.
All inputs are finite; a program needn't handle non-finite values.
Results may differ from a plain program's by a relative error of at most 0.009.
Values may be sent and summed in bfloat16 or wider, within the bound.
A program may use at most 128 MiB of HBM per device.

v0:
```python
import jax
import jax.numpy as jnp
from jax import lax
from jax.sharding import PartitionSpec as P


def from_partner(value, axis, bit):
    mask = 2**bit
    pairs = [(source, source ^ mask) for source in range(lax.axis_size(axis))]
    return lax.ppermute(value, axis, pairs)


def in_blocks(array, dim, count):
    lengths = array.shape
    pieces = array.reshape(*lengths[:dim], count, lengths[dim] // count, *lengths[dim + 1 :])
    return jnp.moveaxis(pieces, dim, 0)


def sum_at_owner(array, axis, dim):
    count = lax.axis_size(axis)
    pieces = lax.all_to_all(in_blocks(array, dim, count), axis, 0, 0, tiled=True)
    return jnp.sum(pieces.astype(jnp.float32), axis=0)


def lift(raw, weight):
    scale = jnp.mean(raw, axis=1, keepdims=True)
    lam = (raw / scale).astype(jnp.bfloat16)
    msg = lax.dot_general(lam, weight, (((1,), (1,)), ((), ())), preferred_element_type=jnp.float32)
    return (lam, msg)


def settle(q_par, lam, msg, weight):
    ratio = (q_par / msg).astype(jnp.bfloat16)
    post = lam.astype(jnp.float32) * jnp.dot(ratio, weight, preferred_element_type=jnp.float32)
    return (ratio, post)


def per_device(mixing, emission, prior, parent, observed):
    node_count = mixing.shape[0]
    states = mixing.shape[1]
    row_count = observed.shape[1]
    values = emission.shape[1]
    levels = lax.axis_size("leaf").bit_length() - 1
    place = lax.axis_index("leaf")
    weights = (
        mixing.astype(jnp.float32) / jnp.sum(mixing.astype(jnp.float32), axis=2, keepdims=True)
    ).astype(jnp.bfloat16)
    tables = (
        emission.astype(jnp.float32) / jnp.sum(emission.astype(jnp.float32), axis=1, keepdims=True)
    ).astype(jnp.bfloat16)
    prior_share = prior / jnp.sum(prior)
    onehots = (observed[:, :, None] == jnp.arange(values, dtype=jnp.int32)[None, None, :]).astype(
        jnp.bfloat16
    )
    emits = jnp.einsum("nrv,nvk->nrk", onehots, tables, preferred_element_type=jnp.float32)
    local_parent = parent - place * node_count
    prods = jnp.ones_like(emits)
    lam_list = [None] * node_count
    msg_list = [None] * node_count
    for node in range(node_count - 1, 0, -1):
        lam, msg = lift(emits[node] * prods[node], weights[node])
        lam_list[node] = lam
        msg_list[node] = msg
        slot = local_parent[node]
        current = lax.dynamic_index_in_dim(prods, slot, 0, keepdims=False)
        prods = lax.dynamic_update_index_in_dim(prods, current * msg, slot, 0)
    block_raw = emits[0] * prods[0]
    block_weight = weights[0]
    stored = []
    for level in range(levels):
        upper = jnp.bitwise_and(place, 1 << level) != 0
        other_raw = from_partner(block_raw, "leaf", level)
        other_weight = from_partner(block_weight, "leaf", level)
        child_raw = jnp.where(upper, block_raw, other_raw)
        child_weight = jnp.where(upper, block_weight, other_weight)
        child_lam, child_msg = lift(child_raw, child_weight)
        stored.append((child_lam, child_msg, child_weight))
        block_raw = jnp.where(upper, other_raw, block_raw) * child_msg
        block_weight = jnp.where(upper, other_weight, block_weight)
    top_lam, top_msg = lift(block_raw, block_weight)
    weighted = prior_share[None, :] * top_msg
    root_share = weighted / jnp.sum(weighted, axis=1, keepdims=True)
    top_ratio, top_post = settle(root_share, top_lam, top_msg, block_weight)
    for level in reversed(range(levels)):
        upper = jnp.bitwise_and(place, 1 << level) != 0
        child_lam, child_msg, child_weight = stored[level]
        ratio, post = settle(top_post, child_lam, child_msg, child_weight)
        top_lam = jnp.where(upper, child_lam, top_lam)
        top_ratio = jnp.where(upper, ratio, top_ratio)
        top_post = jnp.where(upper, post, top_post)
    lam_list[0] = top_lam
    posts = jnp.zeros_like(emits).at[0].set(top_post)
    ratio_list = [top_ratio] + [None] * (node_count - 1)
    for node in range(1, node_count):
        q_par = lax.dynamic_index_in_dim(posts, local_parent[node], 0, keepdims=False)
        ratio, post = settle(q_par, lam_list[node], msg_list[node], weights[node])
        ratio_list[node] = ratio
        posts = posts.at[node].set(post)
    ratio_all = jnp.stack(ratio_list, axis=0)
    lam_all = jnp.stack(lam_list, axis=0)
    post_half = posts.astype(jnp.bfloat16)
    emit_part = jnp.einsum("nrv,nrk->nvk", onehots, post_half, preferred_element_type=jnp.float32)
    groups = lax.axis_size("rows")
    share = states // groups
    spread = lax.all_to_all(ratio_all, "rows", split_axis=2, concat_axis=1, tiled=True)
    flows = jnp.einsum(
        "nra,nrb->nab",
        spread,
        lax.all_gather(lam_all, "rows", axis=1, tiled=True),
        preferred_element_type=jnp.float32,
    )
    emit_sum = sum_at_owner(emit_part.astype(jnp.bfloat16), "rows", 2)
    samples = row_count * groups
    own_rows = lax.dynamic_slice_in_dim(weights, lax.axis_index("rows") * share, share, 1)
    pair_counts = (own_rows.astype(jnp.float32) * flows * (states * states / samples)).astype(
        jnp.bfloat16
    )
    emit_counts = (emit_sum * (values * states / samples)).astype(jnp.bfloat16)
    return (pair_counts, emit_counts)


def solution(mesh):
    placed = (P("leaf", None, None), P("leaf", None, None), P(), P("leaf"), P("leaf", "rows"))
    return jax.shard_map(
        per_device,
        mesh=mesh,
        in_specs=placed,
        out_specs=(P("leaf", "rows", None), P("leaf", None, "rows")),
        check_vma=False,
    )
```

profile of v0, /device:TPU:8, one launch (start us, length us, event | category | flops | bytes accessed | tf_op | source)
XLA Modules:
  0.0 503.5 jit_solution(12902194291016919670)
XLA Ops:
  7.2 3.8 convert_reduce_fusion
  11.8 2.7 fusion
  14.5 2.6 copy-done
  17.4 1.7 convert_reduce_fusion.1
  19.1 2.5 collective-permute-done.1
  21.7 1.8 broadcast_select_fusion.10
  23.5 2.0 collective-permute-start.3
  29.3 1.9 fusion.6
  32.6 3.2 bitcast_dynamic-update-slice_fusion.1
  41.6 30.5 %collective-permute-done.3 = bf16[1024,1024]{1,0:T(8,128)(2,1)} collective-permute-done((bf16[1024,1024]{1,0:T(8,128)(2,1)S(1)}, bf16[1024,1024]{1,0:T(8,128)(2,1)}, u32[]{:S(2)}, u32[]{:S(2)}) %collective-permute-start.3) | collective-permute-done | bytes 2097184 | tf_op jit(solution)/shard_map/ppermute | solution.py:10
  73.7 3.3 collective-permute-start.5
  77.0 3.2 bitcast_dynamic-update-slice_fusion
  81.4 1.9 collective-permute-done
  83.6 3.9 select_multiply_fusion.5
  87.5 3.3 collective-permute-start.2
  90.8 77.3 %collective-permute-done.5 = bf16[1024,1024]{1,0:T(8,128)(2,1)} collective-permute-done((bf16[1024,1024]{1,0:T(8,128)(2,1)}, bf16[1024,1024]{1,0:T(8,128)(2,1)}, u32[]{:S(2)}, u32[]{:S(2)}) %collective-permute-start.5) | collective-permute-done | bytes 2097184 | tf_op jit(solution)/shard_map/ppermute | solution.py:10
  168.1 3.1 broadcast_select_fusion.6
  171.2 6.2 %collective-permute-start.7 = (bf16[1024,1024]{1,0:T(8,128)(2,1)}, bf16[1024,1024]{1,0:T(8,128)(2,1)}, u32[]{:S(2)}, u32[]{:S(2)}) collective-permute-start(bf16[1024,1024]{1,0:T(8,128)(2,1)} %broadcast_select_fusion.6), channel_id=1, source_target_pairs={{0,32},{4,36},{8,40},{12,44},{16,48},{20,52},{24,56},{28,60},{32,0... | collective-permute-start | bytes 6291464 | tf_op jit(solution)/shard_map/ppermute | solution.py:10
  177.7 3.2 select_multiply_fusion.4
  180.9 109.8 %collective-permute-done.4 = f32[128,1024]{1,0:T(8,128)S(1)} collective-permute-done((f32[128,1024]{1,0:T(8,128)S(1)}, f32[128,1024]{1,0:T(8,128)S(1)}, u32[]{:S(2)}, u32[]{:S(2)}) %collective-permute-start.4) | collective-permute-done | bytes 524320 | tf_op jit(solution)/shard_map/ppermute | solution.py:10
  290.9 3.1 broadcast_select_fusion.4
  294.6 3.3 select_multiply_fusion.3
  297.9 3.6 collective-permute-start.6
  301.5 25.1 %collective-permute-done.6 = f32[128,1024]{1,0:T(8,128)S(1)} collective-permute-done((f32[128,1024]{1,0:T(8,128)S(1)}, f32[128,1024]{1,0:T(8,128)S(1)}, u32[]{:S(2)}, u32[]{:S(2)}) %collective-permute-start.6) | collective-permute-done | bytes 524320 | tf_op jit(solution)/shard_map/ppermute | solution.py:10
  326.9 3.4 select_multiply_fusion.2
  331.9 11.0 %collective-permute-done.9 = bf16[1024,1024]{1,0:T(8,128)(2,1)} collective-permute-done((bf16[1024,1024]{1,0:T(8,128)(2,1)}, bf16[1024,1024]{1,0:T(8,128)(2,1)}, u32[]{:S(2)}, u32[]{:S(2)}) %collective-permute-start.9) | collective-permute-done | bytes 2097184 | tf_op jit(solution)/shard_map/ppermute | solution.py:10
  342.9 3.1 broadcast_select_fusion.2
  346.0 2.3 collective-permute-start.11
  348.3 5.7 %collective-permute-done.8 = f32[128,1024]{1,0:T(8,128)S(1)} collective-permute-done((f32[128,1024]{1,0:T(8,128)S(1)}, f32[128,1024]{1,0:T(8,128)S(1)}, u32[]{:S(2)}, u32[]{:S(2)}) %collective-permute-start.8) | collective-permute-done | bytes 524320 | tf_op jit(solution)/shard_map/ppermute | solution.py:10
  354.9 3.4 select_multiply_fusion.1
  358.4 2.3 collective-permute-start.10
  361.9 48.3 %collective-permute-done.10 = f32[128,1024]{1,0:T(8,128)S(1)} collective-permute-done((f32[128,1024]{1,0:T(8,128)S(1)}, f32[128,1024]{1,0:T(8,128)S(1)}, u32[]{:S(2)}, u32[]{:S(2)}) %collective-permute-start.10) | collective-permute-done | bytes 524320 | tf_op jit(solution)/shard_map/ppermute | solution.py:10
  410.6 3.4 fusion.45
  416.0 2.5 multiply_reduce_fusion
  418.6 2.3 divide_convert_fusion.5
  421.0 2.3 divide_convert_fusion.4
  423.3 2.3 divide_convert_fusion.3
  425.6 2.5 divide_convert_fusion.2
  428.2 2.4 divide_convert_fusion.1
  430.6 2.3 fusion.16
  433.9 2.2 select_bitcast_fusion
  437.3 1.7 fusion.10
  440.7 4.3 all-to-all-start
  445.0 2.1 fusion.13
  449.0 18.5 %all-to-all-done = bf16[3,128,1024]{1,0,2:T(4,128)(2,1)S(1)} async-done(((bf16[3,128,1024]{1,0,2:T(4,128)(2,1)}), bf16[3,128,1024]{1,0,2:T(4,128)(2,1)S(1)}, u32[]{:S(2)}, u32[]{:S(2)}) %all-to-all-start) | async-done | bytes 786464 | tf_op jit(solution)/shard_map/all_to_all | solution.py:105
  467.5 3.6 all-to-all-start.1
  474.3 16.8 %all-to-all-done.1 = bf16[4,3,256,256]{3,2,1,0:T(8,128)(2,1)S(1)} async-done(((bf16[4,3,256,256]{3,2,1,0:T(8,128)(2,1)}), bf16[4,3,256,256]{3,2,1,0:T(8,128)(2,1)S(1)}, u32[]{:S(2)}, u32[]{:S(2)}) %all-to-all-start.1) | async-done | bytes 1572896 | tf_op jit(solution)/shard_map/all_to_all | solution.py:21
  492.2 4.5 multiply_convert_fusion
  (133 shorter events, 28.3 us)
Async XLA Ops:
  7.2 485.0 %all-gather.2.cloned.1.call-start = ((), (), s32[]{:S(2)}) async-start(), calls=%async_computation.2 | async-start | bytes 3932160 | tf_op jit(solution)/shard_map/all_gather | solution.py:109
  7.2 4.6 copy-start.1
  14.5 2.6 copy-start
  17.1 2.0 copy-start.34
  17.3 4.4 collective-permute-start.1
  19.1 10.2 %copy-start.33 = (s32[3,128]{1,0:T(4,128)S(1)}, s32[3,128]{1,0:T(4,128)}, u32[]{:S(2)}) copy-start(s32[3,128]{1,0:T(4,128)} %param.15) | copy-start | bytes 4612
  23.5 48.7 %collective-permute-start.3 = (bf16[1024,1024]{1,0:T(8,128)(2,1)S(1)}, bf16[1024,1024]{1,0:T(8,128)(2,1)}, u32[]{:S(2)}, u32[]{:S(2)}) collective-permute-start(bf16[1024,1024]{1,0:T(8,128)(2,1)S(1)} %broadcast_select_fusion.10), channel_id=1, source_target_pairs={{0,8},{4,12},{8,0},{12,4},{16,24},{20,28},{24,16},{28,20},{32,40},... | collective-permute-start | bytes 6291464 | tf_op jit(solution)/shard_map/ppermute | solution.py:10
  31.2 1.2 copy-start.4
  32.4 3.4 copy-start.22
  35.8 1.2 copy-start.2
  41.6 35.4 %copy-start.12 = (bf16[1,128,1024]{2,1,0:T(8,128)(2,1)}, bf16[1,128,1024]{2,1,0:T(8,128)(2,1)S(1)}, u32[]{:S(2)}) copy-start(bf16[1,128,1024]{2,1,0:T(8,128)(2,1)S(1)} %get-tuple-element.50) | copy-start | bytes 786436
  41.6 35.4 %copy-start.8 = (f32[3,128,1024]{2,1,0:T(8,128)S(1)}, f32[3,128,1024]{2,1,0:T(8,128)}, u32[]{:S(2)}) copy-start(f32[3,128,1024]{2,1,0:T(8,128)} %copy.20) | copy-start | bytes 4718596
  73.7 94.4 %collective-permute-start.5 = (bf16[1024,1024]{1,0:T(8,128)(2,1)}, bf16[1024,1024]{1,0:T(8,128)(2,1)}, u32[]{:S(2)}, u32[]{:S(2)}) collective-permute-start(bf16[1024,1024]{1,0:T(8,128)(2,1)} %broadcast_select_fusion.8), channel_id=1, source_target_pairs={{0,16},{4,20},{8,24},{12,28},{16,0},{20,4},{24,8},{28,12},{32,48},... | collective-permute-start | bytes 6291464 | tf_op jit(solution)/shard_map/ppermute | solution.py:10
  81.3 2.0 collective-permute-start
  83.6 4.0 copy-start.9
  87.5 89.9 %collective-permute-start.2 = (f32[128,1024]{1,0:T(8,128)S(1)}, f32[128,1024]{1,0:T(8,128)S(1)}, u32[]{:S(2)}, u32[]{:S(2)}) collective-permute-start(f32[128,1024]{1,0:T(8,128)S(1)} %get-tuple-element.57), channel_id=1, source_target_pairs={{0,8},{4,12},{8,0},{12,4},{16,24},{20,28},{24,16},{28,20},{32,40},... | collective-permute-start | bytes 1572872 | tf_op jit(solution)/shard_map/ppermute | solution.py:10
  171.2 119.7 %collective-permute-start.7 = (bf16[1024,1024]{1,0:T(8,128)(2,1)}, bf16[1024,1024]{1,0:T(8,128)(2,1)}, u32[]{:S(2)}, u32[]{:S(2)}) collective-permute-start(bf16[1024,1024]{1,0:T(8,128)(2,1)} %broadcast_select_fusion.6), channel_id=1, source_target_pairs={{0,32},{4,36},{8,40},{12,44},{16,48},{20,52},{24,56},{28,60},{32,0... | collective-permute-start | bytes 6291464 | tf_op jit(solution)/shard_map/ppermute | solution.py:10
  180.9 109.8 %collective-permute-start.4 = (f32[128,1024]{1,0:T(8,128)S(1)}, f32[128,1024]{1,0:T(8,128)S(1)}, u32[]{:S(2)}, u32[]{:S(2)}) collective-permute-start(f32[128,1024]{1,0:T(8,128)S(1)} %get-tuple-element.59), channel_id=1, source_target_pairs={{0,16},{4,20},{8,24},{12,28},{16,0},{20,4},{24,8},{28,12},{32,48},... | collective-permute-start | bytes 1572872 | tf_op jit(solution)/shard_map/ppermute | solution.py:10
  294.0 48.8 %collective-permute-start.9 = (bf16[1024,1024]{1,0:T(8,128)(2,1)}, bf16[1024,1024]{1,0:T(8,128)(2,1)}, u32[]{:S(2)}, u32[]{:S(2)}) collective-permute-start(bf16[1024,1024]{1,0:T(8,128)(2,1)} %broadcast_select_fusion.4), channel_id=1, source_target_pairs={{0,64},{4,68},{8,72},{12,76},{16,80},{20,84},{24,88},{28,92},{32,9... | collective-permute-start | bytes 6291464 | tf_op jit(solution)/shard_map/ppermute | solution.py:10
  294.6 3.3 copy-start.5
  297.9 28.7 %collective-permute-start.6 = (f32[128,1024]{1,0:T(8,128)S(1)}, f32[128,1024]{1,0:T(8,128)S(1)}, u32[]{:S(2)}, u32[]{:S(2)}) collective-permute-start(f32[128,1024]{1,0:T(8,128)S(1)} %get-tuple-element.61), channel_id=1, source_target_pairs={{0,32},{4,36},{8,40},{12,44},{16,48},{20,52},{24,56},{28,60},{32,0... | collective-permute-start | bytes 1572872 | tf_op jit(solution)/shard_map/ppermute | solution.py:10
  326.9 3.4 copy-start.14
  330.3 23.7 %collective-permute-start.8 = (f32[128,1024]{1,0:T(8,128)S(1)}, f32[128,1024]{1,0:T(8,128)S(1)}, u32[]{:S(2)}, u32[]{:S(2)}) collective-permute-start(f32[128,1024]{1,0:T(8,128)S(1)} %get-tuple-element.63), channel_id=1, source_target_pairs={{0,64},{4,68},{8,72},{12,76},{16,80},{20,84},{24,88},{28,92},{32,9... | collective-permute-start | bytes 1572872 | tf_op jit(solution)/shard_map/ppermute | solution.py:10
  346.0 64.6 %collective-permute-start.11 = (bf16[1024,1024]{1,0:T(8,128)(2,1)}, bf16[1024,1024]{1,0:T(8,128)(2,1)}, u32[]{:S(2)}, u32[]{:S(2)}) collective-permute-start(bf16[1024,1024]{1,0:T(8,128)(2,1)} %broadcast_select_fusion.2), channel_id=1, source_target_pairs={{0,128},{4,132},{8,136},{12,140},{16,144},{20,148},{24,152},{28,15... | collective-permute-start | bytes 6291464 | tf_op jit(solution)/shard_map/ppermute | solution.py:10
  354.9 3.4 copy-start.17
  354.9 5.7 %copy-start.32 = (f32[1024]{0:T(1024)S(1)}, f32[1024]{0:T(1024)}, u32[]{:S(2)}) copy-start(f32[1024]{0:T(1024)} %param.13) | copy-start | bytes 12292
  358.4 51.9 %collective-permute-start.10 = (f32[128,1024]{1,0:T(8,128)S(1)}, f32[128,1024]{1,0:T(8,128)S(1)}, u32[]{:S(2)}, u32[]{:S(2)}) collective-permute-start(f32[128,1024]{1,0:T(8,128)S(1)} %get-tuple-element.65), channel_id=1, source_target_pairs={{0,128},{4,132},{8,136},{12,140},{16,144},{20,148},{24,152},{28,15... | collective-permute-start | bytes 1572872 | tf_op jit(solution)/shard_map/ppermute | solution.py:10
  410.5 3.5 copy-start.20
  410.5 3.5 copy-start.6
  410.5 3.5 copy-start.10
  410.5 3.5 copy-start.15
  410.5 3.5 copy-start.18
  416.0 2.5 copy-start.27
  418.6 2.4 copy-start.21
  418.6 2.4 copy-start.31
  420.9 2.3 copy-start.19
  421.0 2.3 copy-start.30
  423.3 2.3 copy-start.16
  423.3 2.3 copy-start.29
  425.6 2.5 copy-start.7
  425.6 2.5 copy-start.28
  428.2 5.5 %slice-start = ((s8[6291456]{0:T(1024)(128)(4,1)}), s8[4194304]{0:T(1024)(128)(4,1)S(1)}, s32[]{:S(2)}) async-start(s8[6291456]{0:T(1024)(128)(4,1)} %bitcast.126), calls=%async_computation.3 | async-start | bytes 8388608
  430.6 2.3 copy-start.26
  430.6 3.0 slice-start.1
  436.1 1.1 copy-start.24
  437.3 1.8 copy-start.25
  440.7 26.8 %all-to-all-start = ((bf16[3,128,1024]{1,0,2:T(4,128)(2,1)}), bf16[3,128,1024]{1,0,2:T(4,128)(2,1)S(1)}, u32[]{:S(2)}, u32[]{:S(2)}) async-start(bf16[3,128,1024]{1,0,2:T(4,128)(2,1)} %copy.10), calls=%async_computation | async-start | bytes 2097152 | tf_op jit(solution)/shard_map/all_to_all | solution.py:105
  467.5 23.7 %all-to-all-start.1 = ((bf16[4,3,256,256]{3,2,1,0:T(8,128)(2,1)}), bf16[4,3,256,256]{3,2,1,0:T(8,128)(2,1)S(1)}, u32[]{:S(2)}, u32[]{:S(2)}) async-start(bf16[4,3,256,256]{3,2,1,0:T(8,128)(2,1)} %bitcast.124), calls=%async_computation.1 | async-start | bytes 3145728 | tf_op jit(solution)/shard_map/all_to_all | solution.py:21
  (4 other events, 3.8 us)
Sparse Core Ops, SparseCore 0:
  416.1 48.4 all-gather.1
where the time goes:
time: 505 us; the launch traced here: 504 us
  waiting for transfers between devices  347 us (69%)
  matrix products  56.8 us (11%)
  starting transfers between devices  33.1 us (7%)
  other arithmetic  31.1 us (6%)
  between operations  18.7 us (4%)
  local copies, waits for them, and re-layouts  16.4 us (3%)
    ppermute x12, waiting for transfers between devices, from_partner(): return lax.ppermute(value, axis, pairs)  312 us
    dot_general x9, matrix products, lift(): lax.dot_general(lam, weight, (((1,), (1,)), ((), ())), preferred_element_...  29.7 us
    ppermute x12, starting transfers between devices, from_partner(): return lax.ppermute(value, axis, pairs)  25.2 us
    dot_general x9, matrix products, settle(): jnp.dot(ratio, weight, preferred_element_type=jnp.float32)  20.2 us
    all_to_all x1, waiting for transfers between devices, per_device(): lax.all_to_all(ratio_all, 'rows', split_axis=2, concat_axis=1, tiled=True)  18.5 us
    all_to_all x1, waiting for transfers between devices, sum_at_owner(): lax.all_to_all(in_blocks(array, dim, count), axis, 0, 0, tiled=True)  16.8 us
    select_n x5, other arithmetic, per_device(): block_weight = jnp.where(upper, other_weight, block_weight)  12.7 us
  transfers between devices with their start and end apart: 15, of which 11 were waited for; matrix products, arithmetic and copies ran while one was open for 14% of the time, Pallas kernels for 0%

commit v1 on v0

--- a/solution.py
+++ b/solution.py
@@ -102,7 +102,11 @@
     emit_part = jnp.einsum("nrv,nrk->nvk", onehots, post_half, preferred_element_type=jnp.float32)
     groups = lax.axis_size("rows")
     share = states // groups
-    spread = lax.all_to_all(ratio_all, "rows", split_axis=2, concat_axis=1, tiled=True)
+    produce_the_inputs = lambda inner_x, axis_no, which_dim: jnp.concatenate(
+        lax.all_to_all(jnp.stack(jnp.split(inner_x, lax.axis_size("rows"), axis_no)), "rows", 0, 0),
+        which_dim,
+    )
+    spread = produce_the_inputs(ratio_all, 2, 1)
     flows = jnp.einsum(
         "nra,nrb->nab",
         spread,

time: 505 us -> 501 us (level)
  no operation moved by 1% of the time
where the time goes in v1:
time: 501 us; the launch traced here: 499 us
  waiting for transfers between devices  346 us (69%)
  matrix products  56.9 us (11%)
  starting transfers between devices  33.1 us (7%)
  other arithmetic  32.2 us (6%)
  between operations  18.7 us (4%)
  local copies, waits for them, and re-layouts  12.8 us (3%)
    ppermute x12, waiting for transfers between devices, from_partner(): return lax.ppermute(value, axis, pairs)  312 us
    dot_general x9, matrix products, lift(): lax.dot_general(lam, weight, (((1,), (1,)), ((), ())), preferred_element_...  29.6 us
    ppermute x12, starting transfers between devices, from_partner(): return lax.ppermute(value, axis, pairs)  25.2 us
    dot_general x9, matrix products, settle(): jnp.dot(ratio, weight, preferred_element_type=jnp.float32)  20.2 us
    all_to_all x1, waiting for transfers between devices, sum_at_owner(): lax.all_to_all(in_blocks(array, dim, count), axis, 0, 0, tiled=True)  17.7 us
    all_to_all x1, waiting for transfers between devices, per_device(): lax.all_to_all(jnp.stack(jnp.split(inner_x, lax.axis_size('rows'), axis_n...  16 us
    select_n x5, other arithmetic, per_device(): block_weight = jnp.where(upper, other_weight, block_weight)  12.7 us
  transfers between devices with their start and end apart: 15, of which 11 were waited for; matrix products, arithmetic and copies ran while one was open for 14% of the time, Pallas kernels for 0%

profile of v1, /device:TPU:8, one launch (start us, length us, event | category | flops | bytes accessed | tf_op | source)
XLA Modules:
  0.0 499.4 jit_solution(2121275131405130888)
XLA Ops:
  7.2 3.8 convert_reduce_fusion
  11.8 2.7 fusion
  14.5 2.6 copy-done
  17.4 1.7 convert_reduce_fusion.1
  19.1 2.5 collective-permute-done.1
  21.7 1.8 broadcast_select_fusion.10
  23.5 2.0 collective-permute-start.3
  29.3 1.9 fusion.6
  32.6 3.2 bitcast_dynamic-update-slice_fusion.1
  41.6 30.6 %collective-permute-done.3 = bf16[1024,1024]{1,0:T(8,128)(2,1)} collective-permute-done((bf16[1024,1024]{1,0:T(8,128)(2,1)S(1)}, bf16[1024,1024]{1,0:T(8,128)(2,1)}, u32[]{:S(2)}, u32[]{:S(2)}) %collective-permute-start.3) | collective-permute-done | bytes 2097184 | tf_op jit(solution)/shard_map/ppermute | solution.py:10
  73.7 3.3 collective-permute-start.5
  77.0 3.2 bitcast_dynamic-update-slice_fusion
  81.4 1.9 collective-permute-done
  83.6 4.0 select_multiply_fusion.5
  87.5 3.3 collective-permute-start.2
  90.9 77.3 %collective-permute-done.5 = bf16[1024,1024]{1,0:T(8,128)(2,1)} collective-permute-done((bf16[1024,1024]{1,0:T(8,128)(2,1)}, bf16[1024,1024]{1,0:T(8,128)(2,1)}, u32[]{:S(2)}, u32[]{:S(2)}) %collective-permute-start.5) | collective-permute-done | bytes 2097184 | tf_op jit(solution)/shard_map/ppermute | solution.py:10
  168.1 3.1 broadcast_select_fusion.6
  171.2 6.2 %collective-permute-start.7 = (bf16[1024,1024]{1,0:T(8,128)(2,1)}, bf16[1024,1024]{1,0:T(8,128)(2,1)}, u32[]{:S(2)}, u32[]{:S(2)}) collective-permute-start(bf16[1024,1024]{1,0:T(8,128)(2,1)} %broadcast_select_fusion.6), channel_id=1, source_target_pairs={{0,32},{4,36},{8,40},{12,44},{16,48},{20,52},{24,56},{28,60},{32,0... | collective-permute-start | bytes 6291464 | tf_op jit(solution)/shard_map/ppermute | solution.py:10
  177.7 3.2 select_multiply_fusion.4
  180.9 109.8 %collective-permute-done.4 = f32[128,1024]{1,0:T(8,128)S(1)} collective-permute-done((f32[128,1024]{1,0:T(8,128)S(1)}, f32[128,1024]{1,0:T(8,128)S(1)}, u32[]{:S(2)}, u32[]{:S(2)}) %collective-permute-start.4) | collective-permute-done | bytes 524320 | tf_op jit(solution)/shard_map/ppermute | solution.py:10
  290.9 3.1 broadcast_select_fusion.4
  294.6 3.3 select_multiply_fusion.3
  297.9 3.6 collective-permute-start.6
  301.5 25.1 %collective-permute-done.6 = f32[128,1024]{1,0:T(8,128)S(1)} collective-permute-done((f32[128,1024]{1,0:T(8,128)S(1)}, f32[128,1024]{1,0:T(8,128)S(1)}, u32[]{:S(2)}, u32[]{:S(2)}) %collective-permute-start.6) | collective-permute-done | bytes 524320 | tf_op jit(solution)/shard_map/ppermute | solution.py:10
  326.9 3.4 select_multiply_fusion.2
  331.9 11.0 %collective-permute-done.9 = bf16[1024,1024]{1,0:T(8,128)(2,1)} collective-permute-done((bf16[1024,1024]{1,0:T(8,128)(2,1)}, bf16[1024,1024]{1,0:T(8,128)(2,1)}, u32[]{:S(2)}, u32[]{:S(2)}) %collective-permute-start.9) | collective-permute-done | bytes 2097184 | tf_op jit(solution)/shard_map/ppermute | solution.py:10
  342.9 3.1 broadcast_select_fusion.2
  346.0 2.3 collective-permute-start.11
  348.3 5.7 %collective-permute-done.8 = f32[128,1024]{1,0:T(8,128)S(1)} collective-permute-done((f32[128,1024]{1,0:T(8,128)S(1)}, f32[128,1024]{1,0:T(8,128)S(1)}, u32[]{:S(2)}, u32[]{:S(2)}) %collective-permute-start.8) | collective-permute-done | bytes 524320 | tf_op jit(solution)/shard_map/ppermute | solution.py:10
  354.9 3.4 select_multiply_fusion.1
  358.4 2.3 collective-permute-start.10
  362.0 48.2 %collective-permute-done.10 = f32[128,1024]{1,0:T(8,128)S(1)} collective-permute-done((f32[128,1024]{1,0:T(8,128)S(1)}, f32[128,1024]{1,0:T(8,128)S(1)}, u32[]{:S(2)}, u32[]{:S(2)}) %collective-permute-start.10) | collective-permute-done | bytes 524320 | tf_op jit(solution)/shard_map/ppermute | solution.py:10
  410.6 3.4 fusion.45
  416.0 2.5 multiply_reduce_fusion
  418.6 2.3 divide_convert_fusion.5
  421.0 2.3 divide_convert_fusion.4
  423.3 2.3 divide_convert_fusion.3
  425.7 2.5 divide_convert_fusion.2
  428.2 2.4 divide_convert_fusion.1
  430.6 2.3 fusion.16
  433.9 2.2 select_bitcast_fusion
  437.3 1.7 fusion.10
  440.3 4.3 all-to-all-start
  444.6 2.1 fusion.13
  448.6 16.0 %all-to-all-done = bf16[4,3,128,256]{3,2,1,0:T(8,128)(2,1)S(1)} async-done(((bf16[4,3,128,256]{3,2,1,0:T(8,128)(2,1)}), bf16[4,3,128,256]{3,2,1,0:T(8,128)(2,1)S(1)}, u32[]{:S(2)}, u32[]{:S(2)}) %all-to-all-start) | async-done | bytes 786464 | tf_op jit(solution)/shard_map/all_to_all | solution.py:106
  464.7 3.6 all-to-all-start.1
  469.2 17.7 %all-to-all-done.1 = bf16[4,3,256,256]{3,2,1,0:T(8,128)(2,1)S(1)} async-done(((bf16[4,3,256,256]{3,2,1,0:T(8,128)(2,1)}), bf16[4,3,256,256]{3,2,1,0:T(8,128)(2,1)S(1)}, u32[]{:S(2)}, u32[]{:S(2)}) %all-to-all-start.1) | async-done | bytes 1572896 | tf_op jit(solution)/shard_map/all_to_all | solution.py:21
  488.0 4.6 multiply_convert_fusion
  (135 shorter events, 25.8 us)
Async XLA Ops:
  7.2 480.8 %all-gather.2.cloned.1.call-start = ((), (), s32[]{:S(2)}) async-start(), calls=%async_computation.2 | async-start | bytes 3932160 | tf_op jit(solution)/shard_map/all_gather | solution.py:113
  7.2 4.6 copy-start.1
  14.5 2.6 copy-start
  17.1 2.0 copy-start.35
  17.3 4.4 collective-permute-start.1
  19.1 10.2 %copy-start.34 = (s32[3,128]{1,0:T(4,128)S(1)}, s32[3,128]{1,0:T(4,128)}, u32[]{:S(2)}) copy-start(s32[3,128]{1,0:T(4,128)} %param.15) | copy-start | bytes 4612
  23.5 48.7 %collective-permute-start.3 = (bf16[1024,1024]{1,0:T(8,128)(2,1)S(1)}, bf16[1024,1024]{1,0:T(8,128)(2,1)}, u32[]{:S(2)}, u32[]{:S(2)}) collective-permute-start(bf16[1024,1024]{1,0:T(8,128)(2,1)S(1)} %broadcast_select_fusion.10), channel_id=1, source_target_pairs={{0,8},{4,12},{8,0},{12,4},{16,24},{20,28},{24,16},{28,20},{32,40},... | collective-permute-start | bytes 6291464 | tf_op jit(solution)/shard_map/ppermute | solution.py:10
  31.2 1.1 copy-start.4
  32.4 3.4 copy-start.22
  35.8 1.2 copy-start.2
  41.6 35.4 %copy-start.12 = (bf16[1,128,1024]{2,1,0:T(8,128)(2,1)}, bf16[1,128,1024]{2,1,0:T(8,128)(2,1)S(1)}, u32[]{:S(2)}) copy-start(bf16[1,128,1024]{2,1,0:T(8,128)(2,1)S(1)} %get-tuple-element.50) | copy-start | bytes 786436
  41.6 35.4 %copy-start.8 = (f32[3,128,1024]{2,1,0:T(8,128)S(1)}, f32[3,128,1024]{2,1,0:T(8,128)}, u32[]{:S(2)}) copy-start(f32[3,128,1024]{2,1,0:T(8,128)} %copy.21) | copy-start | bytes 4718596
  73.7 94.4 %collective-permute-start.5 = (bf16[1024,1024]{1,0:T(8,128)(2,1)}, bf16[1024,1024]{1,0:T(8,128)(2,1)}, u32[]{:S(2)}, u32[]{:S(2)}) collective-permute-start(bf16[1024,1024]{1,0:T(8,128)(2,1)} %broadcast_select_fusion.8), channel_id=1, source_target_pairs={{0,16},{4,20},{8,24},{12,28},{16,0},{20,4},{24,8},{28,12},{32,48},... | collective-permute-start | bytes 6291464 | tf_op jit(solution)/shard_map/ppermute | solution.py:10
  81.3 2.0 collective-permute-start
  83.6 4.0 copy-start.9
  87.5 89.9 %collective-permute-start.2 = (f32[128,1024]{1,0:T(8,128)S(1)}, f32[128,1024]{1,0:T(8,128)S(1)}, u32[]{:S(2)}, u32[]{:S(2)}) collective-permute-start(f32[128,1024]{1,0:T(8,128)S(1)} %get-tuple-element.61), channel_id=1, source_target_pairs={{0,8},{4,12},{8,0},{12,4},{16,24},{20,28},{24,16},{28,20},{32,40},... | collective-permute-start | bytes 1572872 | tf_op jit(solution)/shard_map/ppermute | solution.py:10
  171.2 119.7 %collective-permute-start.7 = (bf16[1024,1024]{1,0:T(8,128)(2,1)}, bf16[1024,1024]{1,0:T(8,128)(2,1)}, u32[]{:S(2)}, u32[]{:S(2)}) collective-permute-start(bf16[1024,1024]{1,0:T(8,128)(2,1)} %broadcast_select_fusion.6), channel_id=1, source_target_pairs={{0,32},{4,36},{8,40},{12,44},{16,48},{20,52},{24,56},{28,60},{32,0... | collective-permute-start | bytes 6291464 | tf_op jit(solution)/shard_map/ppermute | solution.py:10
  180.9 109.8 %collective-permute-start.4 = (f32[128,1024]{1,0:T(8,128)S(1)}, f32[128,1024]{1,0:T(8,128)S(1)}, u32[]{:S(2)}, u32[]{:S(2)}) collective-permute-start(f32[128,1024]{1,0:T(8,128)S(1)} %get-tuple-element.63), channel_id=1, source_target_pairs={{0,16},{4,20},{8,24},{12,28},{16,0},{20,4},{24,8},{28,12},{32,48},... | collective-permute-start | bytes 1572872 | tf_op jit(solution)/shard_map/ppermute | solution.py:10
  294.0 48.8 %collective-permute-start.9 = (bf16[1024,1024]{1,0:T(8,128)(2,1)}, bf16[1024,1024]{1,0:T(8,128)(2,1)}, u32[]{:S(2)}, u32[]{:S(2)}) collective-permute-start(bf16[1024,1024]{1,0:T(8,128)(2,1)} %broadcast_select_fusion.4), channel_id=1, source_target_pairs={{0,64},{4,68},{8,72},{12,76},{16,80},{20,84},{24,88},{28,92},{32,9... | collective-permute-start | bytes 6291464 | tf_op jit(solution)/shard_map/ppermute | solution.py:10
  294.6 3.3 copy-start.5
  297.9 28.7 %collective-permute-start.6 = (f32[128,1024]{1,0:T(8,128)S(1)}, f32[128,1024]{1,0:T(8,128)S(1)}, u32[]{:S(2)}, u32[]{:S(2)}) collective-permute-start(f32[128,1024]{1,0:T(8,128)S(1)} %get-tuple-element.65), channel_id=1, source_target_pairs={{0,32},{4,36},{8,40},{12,44},{16,48},{20,52},{24,56},{28,60},{32,0... | collective-permute-start | bytes 1572872 | tf_op jit(solution)/shard_map/ppermute | solution.py:10
  326.9 3.4 copy-start.14
  330.3 23.7 %collective-permute-start.8 = (f32[128,1024]{1,0:T(8,128)S(1)}, f32[128,1024]{1,0:T(8,128)S(1)}, u32[]{:S(2)}, u32[]{:S(2)}) collective-permute-start(f32[128,1024]{1,0:T(8,128)S(1)} %get-tuple-element.67), channel_id=1, source_target_pairs={{0,64},{4,68},{8,72},{12,76},{16,80},{20,84},{24,88},{28,92},{32,9... | collective-permute-start | bytes 1572872 | tf_op jit(solution)/shard_map/ppermute | solution.py:10
  346.0 64.6 %collective-permute-start.11 = (bf16[1024,1024]{1,0:T(8,128)(2,1)}, bf16[1024,1024]{1,0:T(8,128)(2,1)}, u32[]{:S(2)}, u32[]{:S(2)}) collective-permute-start(bf16[1024,1024]{1,0:T(8,128)(2,1)} %broadcast_select_fusion.2), channel_id=1, source_target_pairs={{0,128},{4,132},{8,136},{12,140},{16,144},{20,148},{24,152},{28,15... | collective-permute-start | bytes 6291464 | tf_op jit(solution)/shard_map/ppermute | solution.py:10
  354.9 3.4 copy-start.17
  354.9 5.7 %copy-start.33 = (f32[1024]{0:T(1024)S(1)}, f32[1024]{0:T(1024)}, u32[]{:S(2)}) copy-start(f32[1024]{0:T(1024)} %param.13) | copy-start | bytes 12292
  358.4 51.9 %collective-permute-start.10 = (f32[128,1024]{1,0:T(8,128)S(1)}, f32[128,1024]{1,0:T(8,128)S(1)}, u32[]{:S(2)}, u32[]{:S(2)}) collective-permute-start(f32[128,1024]{1,0:T(8,128)S(1)} %get-tuple-element.69), channel_id=1, source_target_pairs={{0,128},{4,132},{8,136},{12,140},{16,144},{20,148},{24,152},{28,15... | collective-permute-start | bytes 1572872 | tf_op jit(solution)/shard_map/ppermute | solution.py:10
  410.5 3.5 copy-start.20
  410.5 3.5 copy-start.6
  410.5 3.5 copy-start.10
  410.5 3.5 copy-start.15
  410.5 3.5 copy-start.18
  416.0 2.5 copy-start.28
  418.6 2.4 copy-start.21
  418.6 2.4 copy-start.32
  421.0 2.3 copy-start.19
  421.0 2.3 copy-start.31
  423.3 2.3 copy-start.16
  423.3 2.3 copy-start.30
  425.6 2.5 copy-start.7
  425.6 2.5 copy-start.29
  428.2 5.4 %slice-start = ((s8[6291456]{0:T(1024)(128)(4,1)}), s8[4194304]{0:T(1024)(128)(4,1)S(1)}, s32[]{:S(2)}) async-start(s8[6291456]{0:T(1024)(128)(4,1)} %bitcast.130), calls=%async_computation.3 | async-start | bytes 8388608
  430.6 2.3 copy-start.26
  430.6 3.0 slice-start.1
  437.3 1.7 copy-start.25
  440.3 24.3 %all-to-all-start = ((bf16[4,3,128,256]{3,2,1,0:T(8,128)(2,1)}), bf16[4,3,128,256]{3,2,1,0:T(8,128)(2,1)S(1)}, u32[]{:S(2)}, u32[]{:S(2)}) async-start(bf16[4,3,128,256]{3,2,1,0:T(8,128)(2,1)} %pad_maximum_fusion.1), calls=%async_computation | async-start | bytes 1572864 | tf_op jit(solution)/shard_map/all_to_all | solution.py:106
  464.7 22.2 %all-to-all-start.1 = ((bf16[4,3,256,256]{3,2,1,0:T(8,128)(2,1)}), bf16[4,3,256,256]{3,2,1,0:T(8,128)(2,1)S(1)}, u32[]{:S(2)}, u32[]{:S(2)}) async-start(bf16[4,3,256,256]{3,2,1,0:T(8,128)(2,1)} %bitcast.129), calls=%async_computation.1 | async-start | bytes 3145728 | tf_op jit(solution)/shard_map/all_to_all | solution.py:21
  469.2 18.8 %copy-start.27 = (bf16[3,4,128,256]{3,2,1,0:T(8,128)(2,1)S(1)}, bf16[3,4,128,256]{3,2,1,0:T(8,128)(2,1)}, u32[]{:S(2)}) copy-start(bf16[3,4,128,256]{3,2,1,0:T(8,128)(2,1)} %copy.12) | copy-start | bytes 2359300
  (5 other events, 4.8 us)
Sparse Core Ops, SparseCore 0:
  416.1 47.9 all-gather.1
